TPU v7x, 1024 devices: a whole 4x4x32 slice. The times are simulated.
1024 devices in a mesh: dp: 64 (over z, core), tensor: 16 (over y, x).
Axes of the slice: x: 4, y: 4, z: 32, core: 2. Of those that a mesh axis runs over, the one named last changes fastest.
Arguments:
- hidden_acts: bfloat16 [49152, 28672], P('dp', 'tensor'), may hold values from -6 to 6
- out_grads: bfloat16 [49152, 8192], P(('dp', 'tensor')), may hold values from -6 to 6
- seq_of_token: int32 [49152], P('dp'), may hold values from 0 to 1, as said below
- proj_in: bfloat16 [28672, 256], P('tensor'), may hold values from -0.046875 to 0.046875
- proj_out: bfloat16 [8192, 128], replicated, may hold values from -0.0034179688 to 0.0034179688
Outputs:
- example_grads: float32 [128, 256, 128], P('dp', 'tensor')
Inputs may be any that keep to these rules, and one draw needn't show every extreme that they name: `seq_of_token`: within the tokens of one index of dp the value never falls, starts at 0, and each of the 2 sequences holds at least one token.
All inputs are finite; a program needn't handle non-finite values.
Results may differ from a plain program's by a relative error of at most 0.0003.
Values may be sent and summed in bfloat16 or wider, within the bound.
A program may use at most 32 MiB of HBM per device.

v0:
```python
import jax
import jax.numpy as jnp
from jax import lax
from jax.experimental import pallas as pl
from jax.experimental.pallas import tpu as pltpu
from jax.sharding import PartitionSpec as P

SEQ_DEV = 2
SIDE = 4
N = SIDE * SIDE
TOK = 768
OWN_TOK = TOK // N
FF_DEV = 1792
D = 8192
K_IN = 256
OWN_K = K_IN // N
K_OUT = 128
ROWS = SEQ_DEV * OWN_K
A_CHUNKS = 3
A_ROWS = TOK // A_CHUNKS
G_CHUNKS = 4
G_COLS = D // G_CHUNKS
OFFSETS = [(dy, dx) for dy in range(SIDE) for dx in range(SIDE)]
MESH = pl.DeviceIdType.MESH


def kernel(acts_hbm, grads_hbm, seq_ref, pin_hbm, pout_hbm, out_ref,
           acts_v, grads_v, pin_v, pout_v, g_all, g_split, m_hi, m_lo, part, recv,
           load_sem, g_send, g_recv, p_send, p_recv):
    me = lax.axis_index("tensor")
    y, x = lax.div(me, SIDE), lax.rem(me, SIDE)

    def peer(dy, dx):
        return lax.rem(y + dy, SIDE) * SIDE + lax.rem(x + dx, SIDE)

    g_loads, a_loads = [], []
    for c in range(G_CHUNKS):
        cols = pl.ds(c * G_COLS, G_COLS)
        g_loads.append((
            pltpu.make_async_copy(grads_hbm.at[:, cols], grads_v.at[:, cols], load_sem.at[2 * c]),
            pltpu.make_async_copy(pout_hbm.at[cols], pout_v.at[cols], load_sem.at[2 * c + 1])))
    for c in range(A_CHUNKS):
        rows = pl.ds(c * A_ROWS, A_ROWS)
        a_loads.append(pltpu.make_async_copy(
            acts_hbm.at[rows], acts_v.at[rows], load_sem.at[2 * G_CHUNKS + c]))
    pin_load = pltpu.make_async_copy(pin_hbm, pin_v, load_sem.at[2 * G_CHUNKS + A_CHUNKS])
    for pair in g_loads:
        for load in pair:
            load.start()
    pin_load.start()
    for load in a_loads:
        load.start()

    barrier = pltpu.get_barrier_semaphore()
    for dy, dx in OFFSETS[1:]:
        pl.semaphore_signal(barrier, inc=1, device_id={"tensor": peer(dy, dx)}, device_id_type=MESH)

    rows_low = jnp.zeros((OWN_TOK, K_OUT), jnp.float32)
    for c, pair in enumerate(g_loads):
        for load in pair:
            load.wait()
        cols = pl.ds(c * G_COLS, G_COLS)
        rows_low += jnp.dot(grads_v[:, cols], pout_v[cols, :], preferred_element_type=jnp.float32)

    def g_slot(index):
        return g_all.at[pl.ds(pl.multiple_of(index * OWN_TOK, 8), OWN_TOK)]

    g_slot(me)[...] = rows_low
    pl.semaphore_wait(barrier, N - 1)
    g_copies = []
    for d, (dy, dx) in enumerate(OFFSETS):
        if d:
            copy = pltpu.make_async_remote_copy(
                src_ref=g_slot(me), dst_ref=g_slot(me), send_sem=g_send.at[d], recv_sem=g_recv.at[d],
                device_id={"tensor": peer(dy, dx)}, device_id_type=MESH)
            copy.start()
            g_copies.append(copy)

    pin_load.wait()
    for c, load in enumerate(a_loads):
        load.wait()
        rows = pl.ds(c * A_ROWS, A_ROWS)
        low = jnp.dot(acts_v[rows, :], pin_v[...], preferred_element_type=jnp.float32).T
        seq = seq_ref[:, rows]
        hi = low.astype(jnp.bfloat16)
        lo = (low - hi.astype(jnp.float32)).astype(jnp.bfloat16)
        for split, value in ((m_hi, hi), (m_lo, lo)):
            wide = value.astype(jnp.float32)
            for s in range(SEQ_DEV):
                masked = jnp.where(seq == s, wide, 0.0).astype(jnp.bfloat16)
                split[:, s, :, rows] = masked.reshape(N, OWN_K, A_ROWS)

    for d, (dy, dx) in enumerate(OFFSETS):
        if d:
            source = lax.rem(y + SIDE - dy, SIDE) * SIDE + lax.rem(x + SIDE - dx, SIDE)
            pltpu.make_async_remote_copy(
                src_ref=g_slot(source), dst_ref=g_slot(source), send_sem=g_send.at[d], recv_sem=g_recv.at[d],
                device_id={"tensor": peer(dy, dx)}, device_id_type=MESH).wait_recv()
    g = g_all[...]
    g_hi = g.astype(jnp.bfloat16)
    g_split[:, :K_OUT] = g_hi
    g_split[:, K_OUT:] = (g - g_hi.astype(jnp.float32)).astype(jnp.bfloat16)

    p_copies = []
    for dy in (2, 1, 3, 0):
        first = lax.rem(y + dy, SIDE) * SIDE
        a_hi = m_hi[pl.ds(first, SIDE)].reshape(SIDE * ROWS, TOK)
        a_lo = m_lo[pl.ds(first, SIDE)].reshape(SIDE * ROWS, TOK)
        both = jnp.dot(a_hi, g_split[...], preferred_element_type=jnp.float32)
        value = both[:, :K_OUT] + both[:, K_OUT:] + jnp.dot(
            a_lo, g_split[:, :K_OUT], preferred_element_type=jnp.float32)
        part[pl.ds(first, SIDE)] = value.reshape(SIDE, ROWS, K_OUT)
        for dx in (2, 1, 3, 0):
            d = dy * SIDE + dx
            if d:
                copy = pltpu.make_async_remote_copy(
                    src_ref=part.at[peer(dy, dx)], dst_ref=recv.at[d], send_sem=p_send.at[d],
                    recv_sem=p_recv.at[d], device_id={"tensor": peer(dy, dx)}, device_id_type=MESH)
                copy.start()
                p_copies.append((d, copy))

    total = part[me]
    for d, copy in p_copies:
        copy.wait_recv()
        total += recv[d]
    out_ref[...] = total.reshape(SEQ_DEV, OWN_K, K_OUT)
    for copy in g_copies:
        copy.wait_send()
    for d, copy in p_copies:
        copy.wait_send()


def shards(hidden_acts, out_grads, seq_of_token, proj_in, proj_out):
    hbm = pl.BlockSpec(memory_space=pl.ANY)
    vmem = pl.BlockSpec(memory_space=pltpu.VMEM)
    bf16, f32 = jnp.bfloat16, jnp.float32
    return pl.pallas_call(
        kernel,
        out_shape=jax.ShapeDtypeStruct((SEQ_DEV, OWN_K, K_OUT), f32),
        in_specs=[hbm, hbm, vmem, hbm, hbm],
        out_specs=vmem,
        scratch_shapes=[
            pltpu.VMEM((TOK, FF_DEV), bf16),
            pltpu.VMEM((OWN_TOK, D), bf16),
            pltpu.VMEM((FF_DEV, K_IN), bf16),
            pltpu.VMEM((D, K_OUT), bf16),
            pltpu.VMEM((TOK, K_OUT), f32),
            pltpu.VMEM((TOK, 2 * K_OUT), bf16),
            pltpu.VMEM((N, SEQ_DEV, OWN_K, TOK), bf16),
            pltpu.VMEM((N, SEQ_DEV, OWN_K, TOK), bf16),
            pltpu.VMEM((N, ROWS, K_OUT), f32),
            pltpu.VMEM((N, ROWS, K_OUT), f32),
            pltpu.SemaphoreType.DMA((2 * G_CHUNKS + A_CHUNKS + 1,)),
            pltpu.SemaphoreType.DMA((N,)),
            pltpu.SemaphoreType.DMA((N,)),
            pltpu.SemaphoreType.DMA((N,)),
            pltpu.SemaphoreType.DMA((N,)),
        ],
        compiler_params=pltpu.CompilerParams(collective_id=0, has_side_effects=True),
    )(hidden_acts, out_grads, seq_of_token.reshape(1, TOK), proj_in, proj_out)


def solution(mesh):
    in_specs = (P("dp", "tensor"), P(("dp", "tensor"), None), P("dp"), P("tensor", None), P())
    out_specs = P("dp", "tensor", None)
    return jax.shard_map(shards, mesh=mesh, in_specs=in_specs, out_specs=out_specs, check_vma=False)
```

profile of v0, /device:TPU:2, one launch (start us, length us, event | category | flops | bytes accessed | tf_op | source)
XLA Modules:
  0.0 31.2 jit_solution(3878339047307151690)
XLA Ops:
  0.0 1.3 %reshape.3.seq_ref = s32[1,768]{1,0:T(1,128)} reshape(s32[768]{0:T(1024)} %param.7) | data formatting | bytes 6144 | tf_op jit(solution)/shard_map/reshape | solution.py:160
  1.3 28.6 %shard_map.55 = f32[2,16,128]{2,1,0:T(8,128)} custom-call(bf16[768,1792]{1,0:T(8,128)(2,1)} %acts_hbm.1, bf16[48,8192]{1,0:T(8,128)(2,1)} %grads_hbm.1, s32[1,768]{1,0:T(1,128)} %reshape.3.seq_ref, bf16[1792,256]{1,0:T(8,128)(2,1)} %pin_hbm.1, bf16[8192,128]{1,0:T(8,128)(2,1)} %pout_hbm.1), custom_call_target="tpu_custom_call" | custom-call | tf_op jit(solution)/shard_map/pallas_call | solution.py:137
  29.8 1.3 %copy.7 = f32[2,16,128]{2,1,0:T(8,128)} copy(f32[2,16,128]{2,1,0:T(8,128)} %shard_map.55) | data formatting | bytes 32768
where the time goes:
time: 31.4 us; the launch traced here: 31.2 us
  Pallas kernels  28.6 us (91%)
  local copies, waits for them, and re-layouts  2.59 us (8%)
    pallas_call x1, Pallas kernels, shards(): pl.pallas_call(kernel, out_shape=jax.ShapeDtypeStruct((SEQ_DEV, OWN_K, K_...  28.6 us
    unnamed x1, local copies, waits for them, and re-layouts  1.32 us
    reshape x1, local copies, waits for them, and re-layouts, shards(): seq_of_token.reshape(1, TOK)  1.27 us

commit v1 on v0

--- a/solution.py
+++ b/solution.py
@@ -20,18 +20,24 @@
 A_ROWS = TOK // A_CHUNKS
 G_CHUNKS = 4
 G_COLS = D // G_CHUNKS
-OFFSETS = [(dy, dx) for dy in range(SIDE) for dx in range(SIDE)]
+OFFSETS = [(dy, dx) for dy in (2, 1, 3, 0) for dx in (2, 1, 3, 0)][:-1]
+OFFSETS.sort(key=lambda o: -min(o[0], SIDE - o[0]) - min(o[1], SIDE - o[1]))
+LATE_LOADS = 2
 MESH = pl.DeviceIdType.MESH
 
 
 def kernel(acts_hbm, grads_hbm, seq_ref, pin_hbm, pout_hbm, out_ref,
-           acts_v, grads_v, pin_v, pout_v, g_all, g_split, m_hi, m_lo, part, recv,
+           acts_v, grads_v, pin_v, pout_v, g_split, m_hi, m_lo, part, recv,
            load_sem, g_send, g_recv, p_send, p_recv):
     me = lax.axis_index("tensor")
     y, x = lax.div(me, SIDE), lax.rem(me, SIDE)
 
     def peer(dy, dx):
         return lax.rem(y + dy, SIDE) * SIDE + lax.rem(x + dx, SIDE)
+
+    barrier = pltpu.get_barrier_semaphore()
+    for dy, dx in OFFSETS:
+        pl.semaphore_signal(barrier, inc=1, device_id={"tensor": peer(dy, dx)}, device_id_type=MESH)
 
     g_loads, a_loads = [], []
     for c in range(G_CHUNKS):
@@ -47,41 +53,39 @@
     for pair in g_loads:
         for load in pair:
             load.start()
-    pin_load.start()
-    for load in a_loads:
-        load.start()
-
-    barrier = pltpu.get_barrier_semaphore()
-    for dy, dx in OFFSETS[1:]:
-        pl.semaphore_signal(barrier, inc=1, device_id={"tensor": peer(dy, dx)}, device_id_type=MESH)
-
     rows_low = jnp.zeros((OWN_TOK, K_OUT), jnp.float32)
     for c, pair in enumerate(g_loads):
         for load in pair:
             load.wait()
+        if c == LATE_LOADS:
+            pin_load.start()
+            for load in a_loads:
+                load.start()
         cols = pl.ds(c * G_COLS, G_COLS)
         rows_low += jnp.dot(grads_v[:, cols], pout_v[cols, :], preferred_element_type=jnp.float32)
 
     def g_slot(index):
-        return g_all.at[pl.ds(pl.multiple_of(index * OWN_TOK, 8), OWN_TOK)]
+        return g_split.at[pl.ds(pl.multiple_of(index * OWN_TOK, 16), OWN_TOK)]
 
-    g_slot(me)[...] = rows_low
+    rows_hi = rows_low.astype(jnp.bfloat16)
+    g_slot(me)[:, :K_OUT] = rows_hi
+    g_slot(me)[:, K_OUT:] = (rows_low - rows_hi.astype(jnp.float32)).astype(jnp.bfloat16)
     pl.semaphore_wait(barrier, N - 1)
     g_copies = []
-    for d, (dy, dx) in enumerate(OFFSETS):
-        if d:
-            copy = pltpu.make_async_remote_copy(
-                src_ref=g_slot(me), dst_ref=g_slot(me), send_sem=g_send.at[d], recv_sem=g_recv.at[d],
-                device_id={"tensor": peer(dy, dx)}, device_id_type=MESH)
-            copy.start()
-            g_copies.append(copy)
+    for dy, dx in OFFSETS:
+        d = dy * SIDE + dx
+        copy = pltpu.make_async_remote_copy(
+            src_ref=g_slot(me), dst_ref=g_slot(me), send_sem=g_send.at[d], recv_sem=g_recv.at[d],
+            device_id={"tensor": peer(dy, dx)}, device_id_type=MESH)
+        copy.start()
+        g_copies.append(copy)
 
     pin_load.wait()
     for c, load in enumerate(a_loads):
         load.wait()
         rows = pl.ds(c * A_ROWS, A_ROWS)
         low = jnp.dot(acts_v[rows, :], pin_v[...], preferred_element_type=jnp.float32).T
-        seq = seq_ref[:, rows]
+        seq = seq_ref[rows][None, :]
         hi = low.astype(jnp.bfloat16)
         lo = (low - hi.astype(jnp.float32)).astype(jnp.bfloat16)
         for split, value in ((m_hi, hi), (m_lo, lo)):
@@ -90,16 +94,12 @@
                 masked = jnp.where(seq == s, wide, 0.0).astype(jnp.bfloat16)
                 split[:, s, :, rows] = masked.reshape(N, OWN_K, A_ROWS)
 
-    for d, (dy, dx) in enumerate(OFFSETS):
-        if d:
-            source = lax.rem(y + SIDE - dy, SIDE) * SIDE + lax.rem(x + SIDE - dx, SIDE)
-            pltpu.make_async_remote_copy(
-                src_ref=g_slot(source), dst_ref=g_slot(source), send_sem=g_send.at[d], recv_sem=g_recv.at[d],
-                device_id={"tensor": peer(dy, dx)}, device_id_type=MESH).wait_recv()
-    g = g_all[...]
-    g_hi = g.astype(jnp.bfloat16)
-    g_split[:, :K_OUT] = g_hi
-    g_split[:, K_OUT:] = (g - g_hi.astype(jnp.float32)).astype(jnp.bfloat16)
+    for dy, dx in OFFSETS:
+        d = dy * SIDE + dx
+        source = lax.rem(y + SIDE - dy, SIDE) * SIDE + lax.rem(x + SIDE - dx, SIDE)
+        pltpu.make_async_remote_copy(
+            src_ref=g_slot(source), dst_ref=g_slot(source), send_sem=g_send.at[d], recv_sem=g_recv.at[d],
+            device_id={"tensor": peer(dy, dx)}, device_id_type=MESH).wait_recv()
 
     p_copies = []
     for dy in (2, 1, 3, 0):
@@ -144,7 +144,6 @@
             pltpu.VMEM((OWN_TOK, D), bf16),
             pltpu.VMEM((FF_DEV, K_IN), bf16),
             pltpu.VMEM((D, K_OUT), bf16),
-            pltpu.VMEM((TOK, K_OUT), f32),
             pltpu.VMEM((TOK, 2 * K_OUT), bf16),
             pltpu.VMEM((N, SEQ_DEV, OWN_K, TOK), bf16),
             pltpu.VMEM((N, SEQ_DEV, OWN_K, TOK), bf16),
@@ -157,7 +156,7 @@
             pltpu.SemaphoreType.DMA((N,)),
         ],
         compiler_params=pltpu.CompilerParams(collective_id=0, has_side_effects=True),
-    )(hidden_acts, out_grads, seq_of_token.reshape(1, TOK), proj_in, proj_out)
+    )(hidden_acts, out_grads, seq_of_token, proj_in, proj_out)
 
 
 def solution(mesh):

time: 31.4 us -> 29.5 us (0.939)
  local copies, waits for them, and re-layouts: 2.59 us -> 1.32 us
  Pallas kernels: 28.6 us -> 27.9 us
    reshape x1 -> x0, local copies, waits for them, and re-layouts: 1.27 us -> none  [shards(): seq_of_token.reshape(1, TOK)]
    pallas_call x1, Pallas kernels: 28.6 us -> 27.9 us  [shards(): pl.pallas_call(kernel, out_shape=jax.ShapeDtypeStruct((SEQ_DEV, OWN_K, K_...]
where the time goes in v1:
time: 29.5 us; the launch traced here: 29.2 us
  Pallas kernels  27.9 us (95%)
  local copies, waits for them, and re-layouts  1.32 us (4%)
    pallas_call x1, Pallas kernels, shards(): pl.pallas_call(kernel, out_shape=jax.ShapeDtypeStruct((SEQ_DEV, OWN_K, K_...  27.9 us
    unnamed x1, local copies, waits for them, and re-layouts  1.32 us

profile of v1, /device:TPU:2, one launch (start us, length us, event | category | flops | bytes accessed | tf_op | source)
XLA Modules:
  0.0 29.2 jit_solution(2647193590884638089)
XLA Ops:
  0.0 27.9 %shard_map.55 = f32[2,16,128]{2,1,0:T(8,128)} custom-call(bf16[768,1792]{1,0:T(8,128)(2,1)} %acts_hbm.1, bf16[48,8192]{1,0:T(8,128)(2,1)} %grads_hbm.1, s32[768]{0:T(1024)} %seq_ref.1, bf16[1792,256]{1,0:T(8,128)(2,1)} %pin_hbm.1, bf16[8192,128]{1,0:T(8,128)(2,1)} %pout_hbm.1), custom_call_target="tpu_custom_call" | custom-call | tf_op jit(solution)/shard_map/pallas_call | solution.py:137
  27.9 1.3 %copy.7 = f32[2,16,128]{2,1,0:T(8,128)} copy(f32[2,16,128]{2,1,0:T(8,128)} %shard_map.55) | data formatting | bytes 32768

commit v2 on v1

--- a/solution.py
+++ b/solution.py
@@ -26,8 +26,8 @@
 MESH = pl.DeviceIdType.MESH
 
 
-def kernel(acts_hbm, grads_hbm, seq_ref, pin_hbm, pout_hbm, out_ref,
-           acts_v, grads_v, pin_v, pout_v, g_split, m_hi, m_lo, part, recv,
+def kernel(acts_hbm, grads_hbm, seq_hbm, pin_hbm, pout_hbm, out_ref,
+           seq_ref, acts_v, grads_v, pin_v, pout_v, g_split, m_hi, m_lo, part, recv,
            load_sem, g_send, g_recv, p_send, p_recv):
     me = lax.axis_index("tensor")
     y, x = lax.div(me, SIDE), lax.rem(me, SIDE)
@@ -50,6 +50,7 @@
         a_loads.append(pltpu.make_async_copy(
             acts_hbm.at[rows], acts_v.at[rows], load_sem.at[2 * G_CHUNKS + c]))
     pin_load = pltpu.make_async_copy(pin_hbm, pin_v, load_sem.at[2 * G_CHUNKS + A_CHUNKS])
+    seq_load = pltpu.make_async_copy(seq_hbm, seq_ref, load_sem.at[2 * G_CHUNKS + A_CHUNKS + 1])
     for pair in g_loads:
         for load in pair:
             load.start()
@@ -58,6 +59,7 @@
         for load in pair:
             load.wait()
         if c == LATE_LOADS:
+            seq_load.start()
             pin_load.start()
             for load in a_loads:
                 load.start()
@@ -80,6 +82,7 @@
         copy.start()
         g_copies.append(copy)
 
+    seq_load.wait()
     pin_load.wait()
     for c, load in enumerate(a_loads):
         load.wait()
@@ -136,10 +139,11 @@
     bf16, f32 = jnp.bfloat16, jnp.float32
     return pl.pallas_call(
         kernel,
-        out_shape=jax.ShapeDtypeStruct((SEQ_DEV, OWN_K, K_OUT), f32),
-        in_specs=[hbm, hbm, vmem, hbm, hbm],
+        out_shape=pltpu.VMEM((SEQ_DEV, OWN_K, K_OUT), f32),
+        in_specs=[hbm] * 5,
         out_specs=vmem,
         scratch_shapes=[
+            pltpu.VMEM((TOK,), jnp.int32),
             pltpu.VMEM((TOK, FF_DEV), bf16),
             pltpu.VMEM((OWN_TOK, D), bf16),
             pltpu.VMEM((FF_DEV, K_IN), bf16),
@@ -149,7 +153,7 @@
             pltpu.VMEM((N, SEQ_DEV, OWN_K, TOK), bf16),
             pltpu.VMEM((N, ROWS, K_OUT), f32),
             pltpu.VMEM((N, ROWS, K_OUT), f32),
-            pltpu.SemaphoreType.DMA((2 * G_CHUNKS + A_CHUNKS + 1,)),
+            pltpu.SemaphoreType.DMA((2 * G_CHUNKS + A_CHUNKS + 2,)),
             pltpu.SemaphoreType.DMA((N,)),
             pltpu.SemaphoreType.DMA((N,)),
             pltpu.SemaphoreType.DMA((N,)),

time: 29.5 us -> 27.5 us (0.932)
  Pallas kernels: 27.9 us -> 26.7 us
  local copies, waits for them, and re-layouts: 1.32 us -> 0.61 us
    pallas_call x1, Pallas kernels: 27.9 us -> 26.7 us  [shards(): pl.pallas_call(kernel, out_shape=pltpu.VMEM((SEQ_DEV, OWN_K, K_OUT), f32)...]
    unnamed x1, local copies, waits for them, and re-layouts: 1.32 us -> 0.61 us
where the time goes in v2:
time: 27.5 us; the launch traced here: 27.4 us
  Pallas kernels  26.7 us (97%)
  local copies, waits for them, and re-layouts  0.61 us (2%)
    pallas_call x1, Pallas kernels, shards(): pl.pallas_call(kernel, out_shape=pltpu.VMEM((SEQ_DEV, OWN_K, K_OUT), f32)...  26.7 us
    unnamed x1, local copies, waits for them, and re-layouts  0.61 us

profile of v2, /device:TPU:2, one launch (start us, length us, event | category | flops | bytes accessed | tf_op | source)
XLA Modules:
  0.0 27.4 jit_solution(3248811641697399535)
XLA Ops:
  0.0 26.7 %shard_map.55 = f32[2,16,128]{2,1,0:T(8,128)S(1)} custom-call(bf16[768,1792]{1,0:T(8,128)(2,1)} %acts_hbm.1, bf16[48,8192]{1,0:T(8,128)(2,1)} %grads_hbm.1, s32[768]{0:T(1024)} %seq_hbm.1, bf16[1792,256]{1,0:T(8,128)(2,1)} %pin_hbm.1, bf16[8192,128]{1,0:T(8,128)(2,1)} %pout_hbm.1), custom_call_target="tpu_custom_call" | custom-call | tf_op jit(solution)/shard_map/pallas_call | solution.py:140
  26.7 0.6 %copy.7 = f32[2,16,128]{2,1,0:T(8,128)} copy(f32[2,16,128]{2,1,0:T(8,128)S(1)} %shard_map.55) | data formatting | bytes 32768

commit v3 on v2

--- a/solution.py
+++ b/solution.py
@@ -18,11 +18,11 @@
 ROWS = SEQ_DEV * OWN_K
 A_CHUNKS = 3
 A_ROWS = TOK // A_CHUNKS
-G_CHUNKS = 4
+G_CHUNKS = 8
 G_COLS = D // G_CHUNKS
 OFFSETS = [(dy, dx) for dy in (2, 1, 3, 0) for dx in (2, 1, 3, 0)][:-1]
 OFFSETS.sort(key=lambda o: -min(o[0], SIDE - o[0]) - min(o[1], SIDE - o[1]))
-LATE_LOADS = 2
+LATE_LOADS = 5
 MESH = pl.DeviceIdType.MESH
 
 
@@ -123,7 +123,7 @@
                 p_copies.append((d, copy))
 
     total = part[me]
-    for d, copy in p_copies:
+    for d, copy in sorted(p_copies, key=lambda item: -OFFSETS.index((item[0] // SIDE, item[0] % SIDE))):
         copy.wait_recv()
         total += recv[d]
     out_ref[...] = total.reshape(SEQ_DEV, OWN_K, K_OUT)

time: 27.5 us -> 27.6 us (level)
  no operation moved by 1% of the time
where the time goes in v3:
time: 27.6 us; the launch traced here: 27.4 us
  Pallas kernels  26.8 us (97%)
  local copies, waits for them, and re-layouts  0.61 us (2%)
    pallas_call x1, Pallas kernels, shards(): pl.pallas_call(kernel, out_shape=pltpu.VMEM((SEQ_DEV, OWN_K, K_OUT), f32)...  26.8 us
    unnamed x1, local copies, waits for them, and re-layouts  0.61 us

profile of v3, /device:TPU:2, one launch (start us, length us, event | category | flops | bytes accessed | tf_op | source)
XLA Modules:
  0.0 27.4 jit_solution(15270809258454660011)
XLA Ops:
  0.0 26.8 %shard_map.55 = f32[2,16,128]{2,1,0:T(8,128)S(1)} custom-call(bf16[768,1792]{1,0:T(8,128)(2,1)} %acts_hbm.1, bf16[48,8192]{1,0:T(8,128)(2,1)} %grads_hbm.1, s32[768]{0:T(1024)} %seq_hbm.1, bf16[1792,256]{1,0:T(8,128)(2,1)} %pin_hbm.1, bf16[8192,128]{1,0:T(8,128)(2,1)} %pout_hbm.1), custom_call_target="tpu_custom_call" | custom-call | tf_op jit(solution)/shard_map/pallas_call | solution.py:140
  26.8 0.6 %copy.7 = f32[2,16,128]{2,1,0:T(8,128)} copy(f32[2,16,128]{2,1,0:T(8,128)S(1)} %shard_map.55) | data formatting | bytes 32768
